TPU v7x, 256 devices: a whole 4x4x8 slice. The times are simulated.
256 devices in a mesh: batch: 4 (over y), lat: 8 (over x, core), lon: 8 (over z).
Axes of the slice: x: 4, y: 4, z: 8, core: 2. Of those that a mesh axis runs over, the one named last changes fastest.
Arguments:
- patches: bfloat16 [4, 16, 24, 128, 640], P('batch', 'lat', 'lon'), may hold values from -6 to 6
- kept_index: int32 [4, 16, 24, 64], P('batch', 'lat', 'lon'), may hold values from 0 to 127, as said below
- kept_count: int32 [4, 16, 24], P('batch', 'lat', 'lon'), may hold values from 32 to 64, as said below
- embed_weight: bfloat16 [640, 1280], P('batch'), may hold values from -0.25 to 0.25
- local_qkv: bfloat16 [1280, 3840], P('batch'), may hold values from -6 to 6
- local_out: bfloat16 [1280, 1280], P('batch'), may hold values from -0.15625 to 0.15625
- global_qkv: bfloat16 [1280, 3840], P('batch'), may hold values from -6 to 6
Outputs:
- mixed: bfloat16 [4, 16, 24, 64, 1280], P('batch', 'lat', 'lon')
Inputs may be any that keep to these rules, and one draw needn't show every extreme that they name: `kept_index`: in each window all 64 entries are distinct offsets; the first kept_count of them are the kept tokens in rising order. `kept_count`: every device holds, in its sample, a window with exactly 64 kept tokens.
All inputs are finite; a program needn't handle non-finite values.
Results may differ from a plain program's by a relative error of at most 0.023.
Values may be sent and summed in bfloat16 or wider, within the bound.
A program may use at most 128 MiB of HBM per device.

v0:
```python
import jax
import jax.numpy as jnp
from jax import lax
from jax.sharding import PartitionSpec as P

HEADS = 8
HD = 160
norm_eps = 1e-05
mask_floor = -1e30


def layer_norm(values):
    centre = values - jnp.mean(values, axis=-1, keepdims=True)
    spread = jnp.mean(centre * centre, axis=-1, keepdims=True)
    return centre * lax.rsqrt(spread + norm_eps)


def product(left_rows, right_rows):
    return jnp.dot(left_rows, right_rows, preferred_element_type=jnp.float32)


def gather_weight(shard):
    rows = shard.shape[0] // lax.axis_size("lat")
    piece = lax.dynamic_slice_in_dim(shard, lax.axis_index("lat") * rows, rows, 0)
    return lax.all_gather(piece, ("batch", "lat"), axis=0, tiled=True)


def attend(proj, keep_mask):
    groups, rows = proj.shape[:2]
    split = proj.reshape(groups, rows, 3, HEADS, HD)
    scores = jnp.einsum(
        "bnhd,bmhd->bhnm", split[:, :, 0], split[:, :, 1], preferred_element_type=jnp.float32
    ) * HD ** (-0.5)
    scores = jnp.where(keep_mask[:, None, None, :], scores, mask_floor)
    scores = scores - jnp.max(scores, axis=-1, keepdims=True)
    weights = jnp.exp(scores)
    probabilities = (weights / jnp.sum(weights, axis=-1, keepdims=True)).astype(jnp.bfloat16)
    blended = jnp.einsum(
        "bhnm,bmhd->bnhd", probabilities, split[:, :, 2], preferred_element_type=jnp.float32
    )
    return blended.astype(jnp.bfloat16).reshape(groups, rows, HEADS * HD)


def body(patches, kept_index, kept_count, embed_weight, local_qkv, local_out, global_qkv):
    lat_windows = patches.shape[1]
    lon_windows = patches.shape[2]
    windows = lat_windows * lon_windows
    tokens = patches.shape[3]
    most = kept_index.shape[3]
    rows = windows * most
    inner = HEADS * HD
    owners = lax.axis_size("lat") * lax.axis_size("lon")
    owned = tokens // owners
    me = lax.axis_index("lat") * lax.axis_size("lon") + lax.axis_index("lon")
    patch_rows = patches.reshape(windows, tokens, patches.shape[4])
    kept = lax.broadcasted_iota(jnp.int32, (windows, most), 1) < kept_count.reshape(windows, 1)
    marks = jnp.where(kept, kept_index.reshape(windows, most), -1)
    all_marks = lax.all_gather(marks, ("lat", "lon"), axis=0, tiled=True)
    wanted = me + owners * lax.broadcasted_iota(jnp.int32, (owned, 1, 1), 0)
    member = jnp.any(all_marks[None] == wanted, axis=-1)
    chosen = (
        marks[:, :, None] == lax.broadcasted_iota(jnp.int32, (windows, most, tokens), 2)
    ).astype(jnp.bfloat16)
    picked = (
        jnp.einsum("wkt,wtd->wkd", chosen, patch_rows, preferred_element_type=jnp.float32)
        .astype(jnp.bfloat16)
        .reshape(rows, -1)
    )
    embedded = product(picked, gather_weight(embed_weight)).astype(jnp.bfloat16)
    normed = layer_norm(embedded.astype(jnp.float32)).astype(jnp.bfloat16)
    local_proj = product(normed, gather_weight(local_qkv)).astype(jnp.bfloat16)
    local_mix = attend(local_proj.reshape(windows, most, -1), kept).reshape(rows, inner)
    hidden = (embedded.astype(jnp.float32) + product(local_mix, gather_weight(local_out))).astype(
        jnp.bfloat16
    )
    normed_global = layer_norm(hidden.astype(jnp.float32)).astype(jnp.bfloat16)
    slots = jnp.einsum(
        "wkt,wkd->twd",
        chosen,
        normed_global.reshape(windows, most, -1),
        preferred_element_type=jnp.float32,
    ).astype(jnp.bfloat16)
    received = lax.all_to_all(
        slots.reshape(owned, owners, windows, -1),
        ("lat", "lon"),
        split_axis=1,
        concat_axis=1,
        tiled=True,
    )
    group = owners * windows
    global_proj = product(received.reshape(owned * group, -1), gather_weight(global_qkv))
    blended = attend(
        global_proj.astype(jnp.bfloat16).reshape(owned, group, -1), member.reshape(owned, group)
    )
    returned = lax.all_to_all(
        blended.reshape(owned, owners, windows, inner),
        ("lat", "lon"),
        split_axis=1,
        concat_axis=1,
        tiled=True,
    ).reshape(tokens, windows, inner)
    result = jnp.einsum(
        "wkt,twd->wkd", chosen, returned, preferred_element_type=jnp.float32
    ).astype(jnp.bfloat16)
    return result.reshape(1, lat_windows, lon_windows, most, inner)


def solution(mesh):
    return jax.shard_map(
        body,
        mesh=mesh,
        in_specs=(
            P("batch", "lat", "lon", None, None),
            P("batch", "lat", "lon", None),
            P("batch", "lat", "lon"),
            P("batch", None),
            P("batch", None),
            P("batch", None),
            P("batch", None),
        ),
        out_specs=P("batch", "lat", "lon", None, None),
        check_vma=False,
    )
```

profile of v0, /device:TPU:1, one launch (start us, length us, event | category | flops | bytes accessed | tf_op | source)
XLA Modules:
  0.0 421.8 jit_solution(6911432130226525416)
XLA Ops:
  6.6 1.7 dynamic-slice_bitcast_fusion
  9.2 1.5 constant_dynamic-slice_fusion.1
  10.8 1.7 constant_dynamic-slice_fusion
  13.2 49.4 %all-gather.13.cloned.1.call-done = bf16[32,20,1280]{2,1,0:T(8,128)(2,1)} async-done(((bf16[1,20,1280]{2,1,0:T(8,128)(2,1)}), bf16[32,20,1280]{2,1,0:T(8,128)(2,1)}) %all-gather.13.cloned.1.call-update) | async-done | bytes 1638416 | tf_op jit(solution)/shard_map/all_gather | solution.py:25
  62.6 2.5 reshape.115
  66.5 59.2 %all-gather.7.cloned.1.call-done = bf16[1280,3840]{1,0:T(8,128)(2,1)} async-done(((bf16[40,3840]{1,0:T(8,128)(2,1)}), bf16[1280,3840]{1,0:T(8,128)(2,1)}) %all-gather.7.cloned.1.call-update) | async-done | bytes 9830416 | tf_op jit(solution)/shard_map/all_gather | solution.py:25
  125.7 9.4 %convolution_convert_fusion.1 = bf16[384,3840]{1,0:T(8,128)(2,1)} fusion(bf16[1280,3840]{1,0:T(8,128)(2,1)} %all-gather.7.cloned.1.call-done, bf16[384,1280]{1,0:T(8,128)(2,1)S(1)} %get-tuple-element.12, f32[384]{0:T(512)S(1)} %add_rsqrt_fusion.1, f32[384]{0:T(512)S(1)} %broadcast_multiply_fusion.1), kind=kOutput, calls=%fused_computation.7 | convolution fusion | flops 3778314240 | bytes 13765632 | tf_op jit(solution)/shard_map/dot_general | solution.py:19
  135.1 9.2 %reshape_reshape.12 = bf16[6,64,3,8,160]{4,3,2,1,0:T(8,128)(2,1)} reshape(bf16[384,3840]{1,0:T(8,128)(2,1)} %convolution_convert_fusion.1) | data formatting | bytes 5898240 | tf_op jit(solution)/shard_map/reshape;reshape | solution.py:30
  144.2 2.8 fusion.34
  149.3 4.0 fusion.21
  153.4 2.3 copy.51
  155.7 2.5 reshape_reshape.13
  158.2 19.7 %all-gather.9.cloned.1.call-done = bf16[1280,1280]{1,0:T(8,128)(2,1)} async-done(((bf16[40,1280]{1,0:T(8,128)(2,1)}), bf16[1280,1280]{1,0:T(8,128)(2,1)}) %all-gather.9.cloned.1.call-update) | async-done | bytes 3276816 | tf_op jit(solution)/shard_map/all_gather | solution.py:25
  177.9 3.8 fusion.36
  183.1 3.3 copy.52
  186.4 9.6 %all-to-all-start = ((bf16[2,64,6,1280]{3,0,2,1:T(2,128)(2,1)}), bf16[2,64,6,1280]{3,0,2,1:T(2,128)(2,1)S(1)}, u32[]{:S(2)}, u32[]{:S(2)}) async-start(bf16[2,64,6,1280]{3,0,2,1:T(2,128)(2,1)} %copy.52), calls=%async_computation | async-start | bytes 3932160 | tf_op jit(solution)/shard_map/all_to_all | solution.py:83
  196.0 83.2 %all-gather.1 = s32[64,6,64]{2,1,0:T(8,128)S(1)} all-gather(s32[1,6,64]{2,1,0:T(8,128)S(1)} %fusion.50), channel_id=1, replica_groups=mesh['batch'=4,'lat'=8,'lon'=8] {'lat','lon'}, dimensions={0}, use_global_device_ids=true | all-gather | bytes 99840 | tf_op jit(solution)/shard_map/all_gather | solution.py:58
  279.5 1.8 copy.53
  281.3 2.8 reshape.111
  284.1 13.2 %convolution_convert_fusion = bf16[768,3840]{1,0:T(8,128)(2,1)} fusion(bf16[768,1280]{1,0:T(8,128)(2,1)S(1)} %reshape.111, bf16[1280,3840]{1,0:T(8,128)(2,1)} %all-gather.11.cloned.1.call-done), kind=kOutput, calls=%fused_computation.6 | convolution fusion | flops 7552696320 | bytes 17694720 | tf_op jit(solution)/shard_map/dot_general | solution.py:19
  297.3 16.6 %reshape.118 = bf16[2,384,3,8,160]{4,3,2,1,0:T(8,128)(2,1)} reshape(bf16[768,3840]{1,0:T(8,128)(2,1)} %convolution_convert_fusion) | data formatting | bytes 11796480 | tf_op jit(solution)/shard_map/reshape;reshape | solution.py:30
  313.9 7.0 %fusion.33 = (bf16[2,384,1,8,160]{4,3,2,1,0:T(8,128)(2,1)}, bf16[2,384,1,8,160]{4,3,2,1,0:T(8,128)(2,1)}, bf16[2,384,1,8,160]{4,3,2,1,0:T(8,128)(2,1)}) fusion(bf16[2,384,3,8,160]{4,3,2,1,0:T(8,128)(2,1)} %reshape.118), kind=kLoop, calls=%fused_computation.64 | loop fusion | bytes 11796480 | tf_op jit(solution)/shard_map/slice | solution.py:39
  320.9 3.8 copy.70
  324.7 4.7 %copy.71 = bf16[2,384,1,8,160]{1,4,3,0,2:T(8,128)(2,1)} copy(bf16[2,384,1,8,160]{4,3,2,1,0:T(8,128)(2,1)} %get-tuple-element.7) | data formatting | bytes 3932160
  329.4 4.8 %copy.69 = bf16[2,384,1,8,160]{1,4,3,0,2:T(8,128)(2,1)} copy(bf16[2,384,1,8,160]{4,3,2,1,0:T(8,128)(2,1)} %get-tuple-element.5) | data formatting | bytes 3932160
  334.2 3.5 fusion.13
  337.7 4.1 fusion.37
  341.8 2.8 convert_bitcast_fusion
  344.6 5.0 %copy.60 = bf16[2,384,8,160]{3,2,0,1:T(8,128)(2,1)} copy(bf16[2,384,8,160]{1,3,2,0:T(8,128)(2,1)} %convert_bitcast_fusion) | data formatting | bytes 3932160 | tf_op jit(solution)/shard_map/convert_element_type | solution.py:41
  349.6 6.9 %reshape_reshape.15 = bf16[2,64,6,1280]{3,0,2,1:T(2,128)(2,1)S(1)} reshape(bf16[2,384,8,160]{3,2,0,1:T(8,128)(2,1)} %copy.60) | data formatting | bytes 3932160 | tf_op jit(solution)/shard_map/reshape;reshape | solution.py:96
  356.4 57.1 %all_to_all.10 = bf16[2,64,6,1280]{3,0,2,1:T(2,128)(2,1)S(1)} all-to-all(bf16[2,64,6,1280]{3,0,2,1:T(2,128)(2,1)S(1)} %reshape_reshape.15), channel_id=1, replica_groups=mesh['batch'=4,'lat'=8,'lon'=8] {'lat','lon'}, dimensions={1} | all-to-all | bytes 3932160 | tf_op jit(solution)/shard_map/all_to_all | solution.py:95
  413.8 1.4 convolution_convert_fusion.3
  (48 shorter events, 7.3 us)
Async XLA Ops:
  6.5 1.8 copy-start
  6.5 6.0 %copy-start.5 = (s32[1,2,3]{2,1,0:T(2,128)S(1)}, s32[1,2,3]{2,1,0:T(2,128)}, u32[]{:S(2)}) copy-start(s32[1,2,3]{2,1,0:T(2,128)} %param.9) | copy-start | bytes 76
  6.5 6.1 %copy-start.4 = (s32[1,2,3,64]{3,1,2,0:T(2,128)S(1)}, s32[1,2,3,64]{3,1,2,0:T(2,128)}, u32[]{:S(2)}) copy-start(s32[1,2,3,64]{3,1,2,0:T(2,128)} %param.8) | copy-start | bytes 4612
  6.5 6.3 %copy-start.3 = (bf16[1,2,3,128,640]{4,3,2,1,0:T(8,128)(2,1)S(1)}, bf16[1,2,3,128,640]{4,3,2,1,0:T(8,128)(2,1)}, u32[]{:S(2)}) copy-start(bf16[1,2,3,128,640]{4,3,2,1,0:T(8,128)(2,1)} %param.7) | copy-start | bytes 2949124
  6.5 56.1 %all-gather.13.cloned.1.call-start = ((), (), s32[]{:S(2)}) async-start(), calls=%async_computation.5 | async-start | bytes 2027520 | tf_op jit(solution)/shard_map/all_gather | solution.py:25
  8.3 117.4 %all-gather.7.cloned.1.call-start = ((), (), s32[]{:S(2)}) async-start(), calls=%async_computation.2 | async-start | bytes 10137600 | tf_op jit(solution)/shard_map/all_gather | solution.py:25
  9.1 168.7 %all-gather.9.cloned.1.call-start = ((), (), s32[]{:S(2)}) async-start(), calls=%async_computation.3 | async-start | bytes 3379200 | tf_op jit(solution)/shard_map/all_gather | solution.py:25
  10.8 273.3 %all-gather.11.cloned.1.call-start = ((), (), s32[]{:S(2)}) async-start(), calls=%async_computation.4 | async-start | bytes 10137600 | tf_op jit(solution)/shard_map/all_gather | solution.py:25
  147.8 1.1 copy-start.6
  186.4 93.1 %all-to-all-start = ((bf16[2,64,6,1280]{3,0,2,1:T(2,128)(2,1)}), bf16[2,64,6,1280]{3,0,2,1:T(2,128)(2,1)S(1)}, u32[]{:S(2)}, u32[]{:S(2)}) async-start(bf16[2,64,6,1280]{3,0,2,1:T(2,128)(2,1)} %copy.52), calls=%async_computation | async-start | bytes 3932160 | tf_op jit(solution)/shard_map/all_to_all | solution.py:83
  337.7 4.1 copy-start.2
  413.6 1.7 copy-start.1
Sparse Core Ops, SparseCore 0:
  10.0 52.6 all-gather.12
  65.2 60.4 all-gather.6
  128.3 49.5 all-gather.8
  180.4 74.4 all-gather.10
where the time goes:
time: 423 us; the launch traced here: 422 us
  blocking collectives  140 us (33%)
  waiting for transfers between devices  128 us (30%)
  local copies, waits for them, and re-layouts  83.2 us (20%)
  matrix products  40.9 us (10%)
  between operations  13.3 us (3%)
  starting transfers between devices  9.74 us (2%)
  other arithmetic  5.86 us (1%)
    all_gather x4, waiting for transfers between devices, gather_weight(): return lax.all_gather(piece, ('batch', 'lat'), axis=0, tiled=True)  128 us
    all_gather x1, blocking collectives, body(): all_marks = lax.all_gather(marks, ('lat', 'lon'), axis=0, tiled=True)  83.2 us
    all_to_all x1, blocking collectives, body(): lax.all_to_all(blended.reshape(owned, owners, windows, inner), ('lat', 'l...  57.1 us
    dot_general x4, matrix products, product(): return jnp.dot(left_rows, right_rows, preferred_element_type=jnp.float32)  27.4 us
    another operation x2, local copies, waits for them, and re-layouts, attend(): split = proj.reshape(groups, rows, 3, HEADS, HD)  25.8 us
    unnamed x22, local copies, waits for them, and re-layouts  18.8 us
    all_to_all x1, starting transfers between devices, body(): lax.all_to_all(slots.reshape(owned, owners, windows, -1), ('lat', 'lon'),...  9.58 us
  transfers between devices with their start and end apart: 5, of which 3 were waited for; matrix products, arithmetic and copies ran while one was open for 13% of the time, Pallas kernels for 0%

commit v1 on v0

--- a/solution.py
+++ b/solution.py
@@ -22,7 +22,12 @@
 def gather_weight(shard):
     rows = shard.shape[0] // lax.axis_size("lat")
     piece = lax.dynamic_slice_in_dim(shard, lax.axis_index("lat") * rows, rows, 0)
-    return lax.all_gather(piece, ("batch", "lat"), axis=0, tiled=True)
+    return jnp.concatenate(
+        lax.all_to_all(
+            jnp.stack([piece] * lax.axis_size(("batch", "lat"))), ("batch", "lat"), 0, 0
+        ),
+        axis=0,
+    )
 
 
 def attend(proj, keep_mask):

time: 423 us -> 592 us (1.40)
  blocking collectives: 140 us -> 209 us
  waiting for transfers between devices: 128 us -> 196 us
  starting transfers between devices: 9.74 us -> 43.8 us
  between operations: 13.3 us -> 0.24 us
  local copies, waits for them, and re-layouts: 83.2 us -> 92.6 us
    all_to_all x0 -> x4, waiting for transfers between devices: none -> 148 us  [gather_weight(): lax.all_to_all(jnp.stack([piece] * lax.axis_size(('batch', 'lat'))), ('ba...]
    all_gather x4 -> x0, waiting for transfers between devices: 128 us -> none  [gather_weight(): return lax.all_gather(piece, ('batch', 'lat'), axis=0, tiled=True)]
    all_gather x1, blocking collectives: 83.2 us -> 153 us  [body(): all_marks = lax.all_gather(marks, ('lat', 'lon'), axis=0, tiled=True)]
    all_to_all x1, waiting for transfers between devices: 0.01 us -> 48 us  [body(): lax.all_to_all(slots.reshape(owned, owners, windows, -1), ('lat', 'lon'),...]
    all_to_all x0 -> x4, starting transfers between devices: none -> 31.8 us  [gather_weight(): lax.all_to_all(jnp.stack([piece] * lax.axis_size(('batch', 'lat'))), ('ba...]
    another operation x0 -> x4, local copies, waits for them, and re-layouts: none -> 12.1 us  [gather_weight(): jnp.stack([piece] * lax.axis_size(('batch', 'lat')))]
    unnamed x22 -> x20, local copies, waits for them, and re-layouts: 18.8 us -> 14.6 us
  transfers between devices with their start and end apart: 5 -> 5, of which waited for: 3 -> 4; matrix products, arithmetic and copies ran while one was open for 13% -> 7% of each run, Pallas kernels for 0% -> 0%
where the time goes in v1:
time: 592 us; the launch traced here: 588 us
  blocking collectives  209 us (35%)
  waiting for transfers between devices  196 us (33%)
  local copies, waits for them, and re-layouts  92.6 us (16%)
  starting transfers between devices  43.8 us (7%)
  matrix products  40.7 us (7%)
    all_gather x1, blocking collectives, body(): all_marks = lax.all_gather(marks, ('lat', 'lon'), axis=0, tiled=True)  153 us
    all_to_all x4, waiting for transfers between devices, gather_weight(): lax.all_to_all(jnp.stack([piece] * lax.axis_size(('batch', 'lat'))), ('ba...  148 us
    all_to_all x1, blocking collectives, body(): lax.all_to_all(blended.reshape(owned, owners, windows, inner), ('lat', 'l...  56.2 us
    all_to_all x1, waiting for transfers between devices, body(): lax.all_to_all(slots.reshape(owned, owners, windows, -1), ('lat', 'lon'),...  48 us
    all_to_all x4, starting transfers between devices, gather_weight(): lax.all_to_all(jnp.stack([piece] * lax.axis_size(('batch', 'lat'))), ('ba...  31.8 us
    dot_general x4, matrix products, product(): return jnp.dot(left_rows, right_rows, preferred_element_type=jnp.float32)  27.3 us
    another operation x2, local copies, waits for them, and re-layouts, attend(): split = proj.reshape(groups, rows, 3, HEADS, HD)  25.7 us
    unnamed x20, local copies, waits for them, and re-layouts  14.6 us
  transfers between devices with their start and end apart: 5, of which 4 were waited for; matrix products, arithmetic and copies ran while one was open for 7% of the time, Pallas kernels for 0%

profile of v1, /device:TPU:1, one launch (start us, length us, event | category | flops | bytes accessed | tf_op | source)
XLA Modules:
  0.0 588.0 jit_solution(9198732285463192850)
XLA Ops:
  2.5 8.6 %all-to-all-start = ((bf16[32,20,1280]{2,1,0:T(8,128)(2,1)}), bf16[32,20,1280]{2,1,0:T(8,128)(2,1)}, u32[]{:S(2)}, u32[]{:S(2)}) async-start(bf16[32,20,1280]{2,1,0:T(8,128)(2,1)} %stack.8), calls=%async_computation | async-start | bytes 3932160 | tf_op jit(solution)/shard_map/all_to_all | solution.py:26
  11.2 27.0 %all-to-all-done = bf16[32,20,1280]{2,1,0:T(8,128)(2,1)} async-done(((bf16[32,20,1280]{2,1,0:T(8,128)(2,1)}), bf16[32,20,1280]{2,1,0:T(8,128)(2,1)}, u32[]{:S(2)}, u32[]{:S(2)}) %all-to-all-start) | async-done | bytes 1638432 | tf_op jit(solution)/shard_map/all_to_all | solution.py:26
  38.2 4.4 stack.9
  42.6 6.4 %all-to-all-start.1 = ((bf16[32,40,3840]{2,1,0:T(8,128)(2,1)}), bf16[32,40,3840]{2,1,0:T(8,128)(2,1)}, u32[]{:S(2)}, u32[]{:S(2)}) async-start(bf16[32,40,3840]{2,1,0:T(8,128)(2,1)} %stack.9), calls=%async_computation.1 | async-start | bytes 19660800 | tf_op jit(solution)/shard_map/all_to_all | solution.py:26
  53.0 113.6 %all-to-all-done.1 = bf16[32,40,3840]{2,1,0:T(8,128)(2,1)} async-done(((bf16[32,40,3840]{2,1,0:T(8,128)(2,1)}), bf16[32,40,3840]{2,1,0:T(8,128)(2,1)}, u32[]{:S(2)}, u32[]{:S(2)}) %all-to-all-start.1) | async-done | bytes 9830432 | tf_op jit(solution)/shard_map/all_to_all | solution.py:26
  168.5 12.0 %all-to-all-start.2 = ((bf16[32,40,1280]{2,1,0:T(8,128)(2,1)}), bf16[32,40,1280]{2,1,0:T(8,128)(2,1)}, u32[]{:S(2)}, u32[]{:S(2)}) async-start(bf16[32,40,1280]{2,1,0:T(8,128)(2,1)} %stack.10), calls=%async_computation.2 | async-start | bytes 6553600 | tf_op jit(solution)/shard_map/all_to_all | solution.py:26
  182.0 9.3 %convolution_convert_fusion.1 = bf16[384,3840]{1,0:T(8,128)(2,1)} fusion(bf16[1280,3840]{1,0:T(8,128)(2,1)} %bitcast.2, bf16[384,1280]{1,0:T(8,128)(2,1)S(1)} %get-tuple-element.12, f32[384]{0:T(512)S(1)} %add_rsqrt_fusion.1, f32[384]{0:T(512)S(1)} %broadcast_multiply_fusion.1), kind=kOutput, calls=%fused_computation.7 | convolution fusion | flops 3778314240 | bytes 13765632 | tf_op jit(solution)/shard_map/dot_general | solution.py:19
  191.3 9.1 %reshape_reshape.12 = bf16[6,64,3,8,160]{4,3,2,1,0:T(8,128)(2,1)} reshape(bf16[384,3840]{1,0:T(8,128)(2,1)} %convolution_convert_fusion.1) | data formatting | bytes 5898240 | tf_op jit(solution)/shard_map/reshape;reshape | solution.py:35
  200.4 2.8 fusion.34
  205.5 3.9 fusion.21
  211.7 2.5 reshape_reshape.13
  214.2 7.2 %all-to-all-done.2 = bf16[32,40,1280]{2,1,0:T(8,128)(2,1)} async-done(((bf16[32,40,1280]{2,1,0:T(8,128)(2,1)}), bf16[32,40,1280]{2,1,0:T(8,128)(2,1)}, u32[]{:S(2)}, u32[]{:S(2)}) %all-to-all-start.2) | async-done | bytes 3276832 | tf_op jit(solution)/shard_map/all_to_all | solution.py:26
  221.5 3.8 fusion.36
  226.6 3.3 copy.52
  229.9 12.0 %all-to-all-start.3 = ((bf16[2,64,6,1280]{3,0,2,1:T(2,128)(2,1)}), bf16[2,64,6,1280]{3,0,2,1:T(2,128)(2,1)S(1)}, u32[]{:S(2)}, u32[]{:S(2)}) async-start(bf16[2,64,6,1280]{3,0,2,1:T(2,128)(2,1)} %copy.52), calls=%async_computation.3 | async-start | bytes 3932160 | tf_op jit(solution)/shard_map/all_to_all | solution.py:88
  242.9 48.0 %all-to-all-done.3 = bf16[2,64,6,1280]{3,0,2,1:T(2,128)(2,1)S(1)} async-done(((bf16[2,64,6,1280]{3,0,2,1:T(2,128)(2,1)}), bf16[2,64,6,1280]{3,0,2,1:T(2,128)(2,1)S(1)}, u32[]{:S(2)}, u32[]{:S(2)}) %all-to-all-start.3) | async-done | bytes 1966112 | tf_op jit(solution)/shard_map/all_to_all | solution.py:88
  290.9 4.4 stack.11
  295.3 4.8 all-to-all-start.4
  300.1 152.7 %all-gather = s32[64,6,64]{2,1,0:T(8,128)S(1)} all-gather(s32[1,6,64]{2,1,0:T(8,128)S(1)} %fusion.50), channel_id=1, replica_groups=mesh['batch'=4,'lat'=8,'lon'=8] {'lat','lon'}, dimensions={0}, use_global_device_ids=true | all-gather | bytes 99840 | tf_op jit(solution)/shard_map/all_gather | solution.py:63
  455.0 2.8 reshape.134
  457.7 13.2 %convolution_convert_fusion = bf16[768,3840]{1,0:T(8,128)(2,1)} fusion(bf16[768,1280]{1,0:T(8,128)(2,1)S(1)} %reshape.134, bf16[1280,3840]{1,0:T(8,128)(2,1)} %bitcast.11), kind=kOutput, calls=%fused_computation.6 | convolution fusion | flops 7552696320 | bytes 17694720 | tf_op jit(solution)/shard_map/dot_general | solution.py:19
  471.0 16.6 %reshape.140 = bf16[2,384,3,8,160]{4,3,2,1,0:T(8,128)(2,1)} reshape(bf16[768,3840]{1,0:T(8,128)(2,1)} %convolution_convert_fusion) | data formatting | bytes 11796480 | tf_op jit(solution)/shard_map/reshape;reshape | solution.py:35
  487.6 7.0 %fusion.33 = (bf16[2,384,1,8,160]{4,3,2,1,0:T(8,128)(2,1)}, bf16[2,384,1,8,160]{4,3,2,1,0:T(8,128)(2,1)}, bf16[2,384,1,8,160]{4,3,2,1,0:T(8,128)(2,1)}) fusion(bf16[2,384,3,8,160]{4,3,2,1,0:T(8,128)(2,1)} %reshape.140), kind=kLoop, calls=%fused_computation.64 | loop fusion | bytes 11796480 | tf_op jit(solution)/shard_map/slice | solution.py:44
  494.5 3.8 copy.70
  498.4 4.7 copy.71
  503.1 4.8 copy.69
  507.9 3.5 fusion.13
  511.3 4.1 fusion.37
  515.5 2.8 convert_bitcast_fusion
  518.2 5.0 copy.60
  523.2 6.9 %reshape_reshape.15 = bf16[2,64,6,1280]{3,0,2,1:T(2,128)(2,1)S(1)} reshape(bf16[2,384,8,160]{3,2,0,1:T(8,128)(2,1)} %copy.60) | data formatting | bytes 3932160 | tf_op jit(solution)/shard_map/reshape;reshape | solution.py:101
  530.1 56.2 %all_to_all.30 = bf16[2,64,6,1280]{3,0,2,1:T(2,128)(2,1)S(1)} all-to-all(bf16[2,64,6,1280]{3,0,2,1:T(2,128)(2,1)S(1)} %reshape_reshape.15), channel_id=1, replica_groups=mesh['batch'=4,'lat'=8,'lon'=8] {'lat','lon'}, dimensions={1} | all-to-all | bytes 3932160 | tf_op jit(solution)/shard_map/all_to_all | solution.py:100
  (48 shorter events, 20.7 us)
Async XLA Ops:
  0.0 11.1 %copy-start = (bf16[320,3840]{1,0:T(8,128)(2,1)S(1)}, bf16[320,3840]{1,0:T(8,128)(2,1)}, u32[]{:S(2)}) copy-start(bf16[320,3840]{1,0:T(8,128)(2,1)} %param.11) | copy-start | bytes 7372804
  2.5 35.7 %all-to-all-start = ((bf16[32,20,1280]{2,1,0:T(8,128)(2,1)}), bf16[32,20,1280]{2,1,0:T(8,128)(2,1)}, u32[]{:S(2)}, u32[]{:S(2)}) async-start(bf16[32,20,1280]{2,1,0:T(8,128)(2,1)} %stack.8), calls=%async_computation | async-start | bytes 3932160 | tf_op jit(solution)/shard_map/all_to_all | solution.py:26
  42.6 6.4 %copy-start.5 = (s32[1,2,3]{2,1,0:T(2,128)S(1)}, s32[1,2,3]{2,1,0:T(2,128)}, u32[]{:S(2)}) copy-start(s32[1,2,3]{2,1,0:T(2,128)} %param.9) | copy-start | bytes 76
  42.6 6.5 %copy-start.4 = (s32[1,2,3,64]{3,1,2,0:T(2,128)S(1)}, s32[1,2,3,64]{3,1,2,0:T(2,128)}, u32[]{:S(2)}) copy-start(s32[1,2,3,64]{3,1,2,0:T(2,128)} %param.8) | copy-start | bytes 4612
  42.6 7.6 %copy-start.3 = (bf16[1,2,3,128,640]{4,3,2,1,0:T(8,128)(2,1)S(1)}, bf16[1,2,3,128,640]{4,3,2,1,0:T(8,128)(2,1)}, u32[]{:S(2)}) copy-start(bf16[1,2,3,128,640]{4,3,2,1,0:T(8,128)(2,1)} %param.7) | copy-start | bytes 2949124
  42.6 124.0 %all-to-all-start.1 = ((bf16[32,40,3840]{2,1,0:T(8,128)(2,1)}), bf16[32,40,3840]{2,1,0:T(8,128)(2,1)}, u32[]{:S(2)}, u32[]{:S(2)}) async-start(bf16[32,40,3840]{2,1,0:T(8,128)(2,1)} %stack.9), calls=%async_computation.1 | async-start | bytes 19660800 | tf_op jit(solution)/shard_map/all_to_all | solution.py:26
  168.5 52.9 %all-to-all-start.2 = ((bf16[32,40,1280]{2,1,0:T(8,128)(2,1)}), bf16[32,40,1280]{2,1,0:T(8,128)(2,1)}, u32[]{:S(2)}, u32[]{:S(2)}) async-start(bf16[32,40,1280]{2,1,0:T(8,128)(2,1)} %stack.10), calls=%async_computation.2 | async-start | bytes 6553600 | tf_op jit(solution)/shard_map/all_to_all | solution.py:26
  203.9 1.2 copy-start.6
  229.9 60.9 %all-to-all-start.3 = ((bf16[2,64,6,1280]{3,0,2,1:T(2,128)(2,1)}), bf16[2,64,6,1280]{3,0,2,1:T(2,128)(2,1)S(1)}, u32[]{:S(2)}, u32[]{:S(2)}) async-start(bf16[2,64,6,1280]{3,0,2,1:T(2,128)(2,1)} %copy.52), calls=%async_computation.3 | async-start | bytes 3932160 | tf_op jit(solution)/shard_map/all_to_all | solution.py:88
  295.3 162.4 %all-to-all-start.4 = ((bf16[32,40,3840]{2,1,0:T(8,128)(2,1)}), bf16[32,40,3840]{2,1,0:T(8,128)(2,1)}, u32[]{:S(2)}, u32[]{:S(2)}) async-start(bf16[32,40,3840]{2,1,0:T(8,128)(2,1)} %stack.11), calls=%async_computation.4 | async-start | bytes 19660800 | tf_op jit(solution)/shard_map/all_to_all | solution.py:26
  511.3 4.1 copy-start.2
  586.3 1.7 copy-start.1
